TPU v7x, 128 devices: a whole 4x4x4 slice. The times are simulated.
128 devices in a mesh: pts: 8 (over x, core), snap: 16 (over z, y).
Axes of the slice: x: 4, y: 4, z: 4, core: 2. Of those that a mesh axis runs over, the one named last changes fastest.
Arguments:
- snapshots: bfloat16 [1024, 3, 65536], P('snap', None, 'pts')
- block_starts: int32 [31], replicated, may hold values from 0 to 960, as said below
- point_slab: int32 [65536], P(('pts', 'snap')), may hold values from 0 to 15
- slab_weight: float32 [16], replicated, may hold values from 1 to 10
Outputs:
- mode_field: bfloat16 [2, 33, 31, 3, 65536], P(None, None, None, None, ('pts', 'snap'))
- r_factor: float32 [2, 33, 31, 31], replicated
Inputs may be any that keep to these rules, and one draw needn't show every extreme that they name: `block_starts`: strictly increasing; the first is 0 and the last is 960; neighbours lie more than 16 apart.
All inputs are finite; a program needn't handle non-finite values.
Results may differ from a plain program's by a relative error of at most 0.0017.
The roundings to bfloat16 on the way count: a program that leaves them out, or rounds other values in their place, can miss the bound.
Values may be sent and summed in bfloat16 or wider, within the bound.
No kernel may reach another device: no remote copies, remote signals or barrier semaphores. Data moves between devices by JAX's collectives and lax.ppermute only.
A program may use at most 128 MiB of HBM per device.

v0:
```python
import math

import jax
import jax.numpy as jnp
from jax import lax
from jax.sharding import PartitionSpec as P

NT = 1024
WIN = 64


def make_tables(length, freq_count):
    steps_time = jnp.arange(length, dtype=jnp.int32)
    freq_index = jnp.arange(freq_count, dtype=jnp.int32)
    phase_index = freq_index[:, None] * steps_time[None, :] % length
    angle_value = 2.0 * math.pi / length * phase_index.astype(jnp.float32)
    window = 0.5 - 0.5 * jnp.cos(2.0 * math.pi / length * steps_time.astype(jnp.float32))
    dft_table = jnp.stack(
        [window[None, :] * jnp.cos(angle_value), -window[None, :] * jnp.sin(angle_value)]
    ).astype(jnp.bfloat16)
    row_sums = jnp.sum(dft_table.astype(jnp.float32), axis=2)
    return (dft_table, row_sums)


def spectra(series, starts, dft_table, row_sums):
    blocks = jax.vmap(lambda offset: lax.dynamic_slice_in_dim(series, offset, WIN, 0))(starts)
    raw_spec = jnp.einsum("kfw,bwcp->kfbcp", dft_table, blocks, preferred_element_type=jnp.float32)
    time_mean = jnp.sum(series.astype(jnp.float32), axis=0) / NT
    return raw_spec - row_sums[:, :, None, None, None] * time_mean[None, None, None]


def gram(amplitude):
    highest = lax.Precision.HIGHEST
    amp_real, amp_imag = (amplitude[0], amplitude[1])
    part_real = jnp.einsum("fbn,fdn->bdf", amp_real, amp_real, precision=highest) + jnp.einsum(
        "fbn,fdn->bdf", amp_imag, amp_imag, precision=highest
    )
    part_imag = jnp.einsum("fbn,fdn->bdf", amp_real, amp_imag, precision=highest) - jnp.einsum(
        "fbn,fdn->bdf", amp_imag, amp_real, precision=highest
    )
    return (part_real, part_imag)


def complex_cholesky(gram_real, gram_imag):
    size_n = gram_real.shape[0]
    positions = jnp.arange(size_n, dtype=jnp.int32)
    rows_real = []
    rows_imag = []
    for column in range(size_n):
        rest_real = gram_real[column]
        rest_imag = gram_imag[column]
        if column > 0:
            done_real = jnp.stack(rows_real)
            done_imag = jnp.stack(rows_imag)
            above_real = done_real[:, column]
            above_imag = done_imag[:, column]
            rest_real = rest_real - jnp.sum(
                above_real[:, None] * done_real + above_imag[:, None] * done_imag, axis=0
            )
            rest_imag = rest_imag - jnp.sum(
                above_real[:, None] * done_imag - above_imag[:, None] * done_real, axis=0
            )
        pivot_value = jnp.sqrt(rest_real[column])
        keep_real = (positions >= column)[:, None]
        keep_imag = (positions > column)[:, None]
        rows_real.append(jnp.where(keep_real, rest_real / pivot_value, jnp.zeros_like(rest_real)))
        rows_imag.append(jnp.where(keep_imag, rest_imag / pivot_value, jnp.zeros_like(rest_imag)))
    return (jnp.stack(rows_real), jnp.stack(rows_imag))


def upper_inverse(upper_real, upper_imag):
    size_n = upper_real.shape[0]
    identity = jnp.eye(size_n, dtype=upper_real.dtype)
    rows_real = []
    rows_imag = []
    for row_index in reversed(range(size_n)):
        rest_real = jnp.broadcast_to(identity[row_index][:, None], upper_real.shape[1:])
        rest_imag = jnp.zeros_like(rest_real)
        if row_index < size_n - 1:
            done_real = jnp.stack(rows_real[::-1])
            done_imag = jnp.stack(rows_imag[::-1])
            coef_real = upper_real[row_index, row_index + 1 :]
            coef_imag = upper_imag[row_index, row_index + 1 :]
            rest_real = rest_real - jnp.sum(
                coef_real[:, None] * done_real - coef_imag[:, None] * done_imag, axis=0
            )
            rest_imag = rest_imag - jnp.sum(
                coef_real[:, None] * done_imag + coef_imag[:, None] * done_real, axis=0
            )
        pivot_value = upper_real[row_index, row_index]
        rows_real.append(rest_real / pivot_value)
        rows_imag.append(rest_imag / pivot_value)
    return (jnp.stack(rows_real[::-1]), jnp.stack(rows_imag[::-1]))


def project(amplitude, inv_real, inv_imag):
    highest = lax.Precision.HIGHEST
    amp_real, amp_imag = (amplitude[0], amplitude[1])
    mode_real = jnp.einsum("fbn,bmf->fmn", amp_real, inv_real, precision=highest) - jnp.einsum(
        "fbn,bmf->fmn", amp_imag, inv_imag, precision=highest
    )
    mode_imag = jnp.einsum("fbn,bmf->fmn", amp_real, inv_imag, precision=highest) + jnp.einsum(
        "fbn,bmf->fmn", amp_imag, inv_real, precision=highest
    )
    return jnp.stack([mode_real, mode_imag])


def on_device(snapshots, block_starts, point_slab, slab_weight):
    dft_table, row_sums = make_tables(WIN, WIN // 2 + 1)
    series = lax.all_to_all(snapshots, "snap", split_axis=2, concat_axis=0, tiled=True)
    spectrum = spectra(series, block_starts, dft_table, row_sums)
    freq_count = spectrum.shape[1]
    block_count = spectrum.shape[2]
    points = spectrum.shape[4]
    all_points = points * lax.axis_size("pts") * lax.axis_size("snap")
    slab_ids = jnp.arange(slab_weight.shape[0], dtype=jnp.int32)
    one_hot = (point_slab[:, None] == slab_ids[None, :]).astype(jnp.float32)
    weights = jnp.dot(one_hot, slab_weight, precision=lax.Precision.HIGHEST)
    root_weight = jnp.sqrt(weights / (0.375 * WIN))
    amplitude = (spectrum * root_weight).reshape(2, freq_count, block_count, 3 * points)
    part_real, part_imag = gram(amplitude)
    norm_scale = 1.0 / (3.0 * all_points)
    sum_real, sum_imag = lax.psum((part_real, part_imag), ("pts", "snap"))
    upper_real, upper_imag = complex_cholesky(sum_real * norm_scale, sum_imag * norm_scale)
    inv_real, inv_imag = upper_inverse(upper_real, upper_imag)
    mode_field = (
        project(amplitude, inv_real, inv_imag)
        .reshape(2, freq_count, block_count, 3, points)
        .astype(jnp.bfloat16)
    )
    r_factor = jnp.transpose(jnp.stack([upper_real, upper_imag]), (0, 3, 1, 2))
    return (mode_field, r_factor)


def solution(mesh):
    in_specs = (P("snap", None, "pts"), P(), P(("pts", "snap")), P())
    out_specs = (P(None, None, None, None, ("pts", "snap")), P())
    return jax.shard_map(
        on_device, mesh=mesh, in_specs=in_specs, out_specs=out_specs, check_vma=False
    )
```

profile of v0, /device:TPU:1, one launch (start us, length us, event | category | flops | bytes accessed | tf_op | source)
XLA Modules:
  0.0 542.6 jit_solution(6044256804985214735)
XLA Ops:
  7.2 11.3 %copy.17234 = bf16[64,3,8192]{0,1,2:T(4,128)(2,1)} copy(bf16[64,3,8192]{2,0,1:T(8,128)(2,1)} %param.4) | data formatting | bytes 6291456 | tf_op args[0]
  18.4 13.4 %reshape.4626 = bf16[16,2,49152]{2,1,0:T(2,128)(2,1)} reshape(bf16[8192,3,64]{2,1,0:T(4,128)(2,1)} %bitcast.635) | data formatting | bytes 6291456
  31.8 8.6 %all-to-all-start = ((bf16[16,2,49152]{2,1,0:T(2,128)(2,1)}), bf16[16,2,49152]{2,1,0:T(2,128)(2,1)S(1)}, u32[]{:S(2)}, u32[]{:S(2)}) async-start(bf16[16,2,49152]{2,1,0:T(2,128)(2,1)} %reshape.4626), calls=%async_computation | async-start | bytes 6291456 | tf_op jit(solution)/shard_map/all_to_all | solution.py:110
  41.5 45.5 %all-to-all-done = bf16[16,2,49152]{2,1,0:T(2,128)(2,1)S(1)} async-done(((bf16[16,2,49152]{2,1,0:T(2,128)(2,1)}), bf16[16,2,49152]{2,1,0:T(2,128)(2,1)S(1)}, u32[]{:S(2)}, u32[]{:S(2)}) %all-to-all-start) | async-done | bytes 3145760 | tf_op jit(solution)/shard_map/all_to_all | solution.py:110
  87.0 9.3 %reshape.4627 = bf16[8192,3,64]{2,1,0:T(4,128)(2,1)} reshape(bf16[16,2,49152]{2,1,0:T(2,128)(2,1)S(1)} %all-to-all-done) | data formatting | bytes 6291456
  96.3 8.3 %copy.17846 = bf16[64,3,16,512]{3,2,0,1:T(8,128)(2,1)S(1)} copy(bf16[64,3,16,512]{0,1,3,2:T(4,128)(2,1)} %bitcast.634) | data formatting | bytes 6291456 | tf_op jit(solution)/shard_map/all_to_all | solution.py:110
  110.2 11.6 %gather_fusion = bf16[31,64,3,512]{3,2,1,0:T(4,128)(2,1)} fusion(bf16[1024,3,512]{2,1,0:T(4,128)(2,1)} %bitcast.633, s32[31]{0:T(128)S(1)} %fusion.108), kind=kCustom, calls=%fused_computation | custom fusion | bytes 12190068 | tf_op jit(solution)/shard_map/vmap()/gather | solution.py:26
  121.8 11.4 %subtract_multiply_fusion = f32[2,33,31,3,512]{4,1,3,2,0:T(8,128)} fusion(f32[512]{0:T(512)S(1)} %multiply_sqrt_fusion, f32[2,33,3,512]{3,1,2,0:T(8,128)S(1)} %broadcast_multiply_fusion.2, bf16[31,64,3,512]{3,2,1,0:T(4,128)(2,1)} %gather_fusion, bf16[1,33,64]{2,1,0:T(8,128)(2,1)S(1)} %get-tuple-element.379, bf16[1,33,64]{2,1,0:T(8,128)(2,1)S(1)} %get-tuple-element.380), kind=kOutput, calls=%fused_computation.1 | convolution fusion | flops 408562176 | bytes 19081472 | tf_op jit(solution)/shard_map/kfw,bwcp->kfbcp/dot_general | solution.py:27
  133.2 12.5 %fusion.116 = (f32[1,33,31,3,512]{4,1,3,2,0:T(8,128)}, f32[1,33,31,3,512]{4,1,3,2,0:T(8,128)}) fusion(f32[2,33,31,3,512]{4,1,3,2,0:T(8,128)} %subtract_multiply_fusion), kind=kLoop, calls=%fused_computation.928 | loop fusion | bytes 25141248 | tf_op jit(solution)/shard_map/slice | solution.py:34
  145.7 10.7 %copy.17238 = f32[1,33,31,3,512]{4,3,2,1,0:T(4,128)} copy(f32[1,33,31,3,512]{4,1,3,2,0:T(8,128)} %get-tuple-element.190) | data formatting | bytes 12570624 | tf_op jit(solution)/shard_map/slice | solution.py:34
  156.4 11.8 %squeeze.62 = f32[33,31,1536]{2,1,0:T(8,128)} reshape(f32[1,33,31,3,512]{4,3,2,1,0:T(4,128)} %copy.17238) | data formatting | bytes 12570624 | tf_op jit(solution)/shard_map/squeeze | solution.py:34
  168.2 10.7 %copy.17239 = f32[1,33,31,3,512]{4,3,2,1,0:T(4,128)} copy(f32[1,33,31,3,512]{4,1,3,2,0:T(8,128)} %get-tuple-element.191) | data formatting | bytes 12570624 | tf_op jit(solution)/shard_map/slice | solution.py:34
  178.9 11.4 %squeeze.63 = f32[33,31,1536]{2,1,0:T(8,128)} reshape(f32[1,33,31,3,512]{4,3,2,1,0:T(4,128)} %copy.17239) | data formatting | bytes 12570624 | tf_op jit(solution)/shard_map/squeeze | solution.py:34
  190.4 9.4 %fusion.123 = f32[33,31,31]{2,1,0:T(8,128)S(1)} fusion(f32[33,31,1536]{2,1,0:T(8,128)} %squeeze.62, f32[33,31,1536]{2,1,0:T(8,128)} %squeeze.63), kind=kOutput, calls=%fused_computation.935 | convolution fusion | flops 584534016 | bytes 12697476 | tf_op jit(solution)/shard_map/fbn,fdn->bdf/dot_general | solution.py:38
  205.7 6.4 %fusion.120 = f32[33,31,31]{2,1,0:T(8,128)S(1)} fusion(f32[33,31,1536]{2,1,0:T(8,128)S(1)} %copy-done.2), kind=kOutput, calls=%fused_computation.932 | convolution fusion | flops 584534016 | bytes 6412164 | tf_op jit(solution)/shard_map/fbn,fdn->bdf/dot_general | solution.py:35
  212.1 6.1 %fusion.121 = f32[33,31,31]{2,1,0:T(8,128)S(1)} fusion(f32[33,31,1536]{2,1,0:T(8,128)S(1)} %copy-done.3), kind=kOutput, calls=%fused_computation.933 | convolution fusion | flops 584534016 | bytes 6412164 | tf_op jit(solution)/shard_map/fbn,fdn->bdf/dot_general | solution.py:35
  221.9 147.2 %all-reduce.4.cloned.1.call-done = (f32[31,31,33]{2,0,1:T(8,128)}, f32[31,31,33]{2,0,1:T(8,128)}) async-done(((f32[31,31,33]{2,0,1:T(8,128)}, f32[31,31,33]{2,0,1:T(8,128)}), (f32[31,31,33]{2,0,1:T(8,128)}, f32[31,31,33]{2,0,1:T(8,128)})) %all-reduce.4.cloned.1.call-update) | async-done | bytes 253720 | tf_op jit(solution)/shard_map/psum | solution.py:123
  466.6 9.6 %fusion.124 = f32[33,31,1536]{2,1,0:T(8,128)} fusion(f32[31,31,33]{0,1,2:T(8,128)S(1)} %copy.17831, f32[33,31,1536]{2,1,0:T(8,128)} %squeeze.62), kind=kOutput, calls=%fused_computation.936 | convolution fusion | flops 584534016 | bytes 12697476 | tf_op jit(solution)/shard_map/fbn,bmf->fmn/dot_general | solution.py:99
  477.7 9.6 %fusion.125 = f32[33,31,1536]{2,1,0:T(8,128)} fusion(f32[31,31,33]{0,1,2:T(8,128)S(1)} %copy.17835, f32[33,31,1536]{2,1,0:T(8,128)} %squeeze.62), kind=kOutput, calls=%fused_computation.937 | convolution fusion | flops 584534016 | bytes 12697476 | tf_op jit(solution)/shard_map/fbn,bmf->fmn/dot_general | solution.py:102
  487.2 9.5 %subtract_convert_fusion = bf16[33,31,1536]{2,1,0:T(8,128)(2,1)} fusion(f32[33,31,1536]{2,1,0:T(8,128)S(1)} %bitcast.638, f32[31,31,33]{0,1,2:T(8,128)S(1)} %copy.17835, f32[33,31,1536]{2,1,0:T(8,128)} %squeeze.63), kind=kOutput, calls=%fused_computation.4 | convolution fusion | flops 587676672 | bytes 15840132 | tf_op jit(solution)/shard_map/fbn,bmf->fmn/dot_general | solution.py:99
  496.8 8.7 %stack.380 = bf16[1,33,31,3,512]{4,3,2,1,0:T(4,128)(2,1)} reshape(bf16[33,31,1536]{2,1,0:T(8,128)(2,1)} %subtract_convert_fusion) | data formatting | bytes 6285312 | tf_op jit(solution)/shard_map/stack | solution.py:105
  505.5 8.9 %add_convert_fusion = bf16[33,31,1536]{2,1,0:T(8,128)(2,1)S(1)} fusion(f32[33,31,1536]{2,1,0:T(8,128)} %fusion.125, f32[31,31,33]{0,1,2:T(8,128)} %copy-done.5, f32[33,31,1536]{2,1,0:T(8,128)} %squeeze.63), kind=kOutput, calls=%fused_computation.3 | convolution fusion | flops 587676672 | bytes 15840132 | tf_op jit(solution)/shard_map/fbn,bmf->fmn/dot_general | solution.py:102
  520.2 7.6 %pad_maximum_fusion = bf16[2,33,31,3,512]{4,3,2,1,0:T(4,128)(2,1)S(1)} fusion(bf16[1,33,31,3,512]{4,3,2,1,0:T(4,128)(2,1)} %stack.381, bf16[1,33,31,3,512]{4,3,2,1,0:T(4,128)(2,1)} %stack.380), kind=kLoop, calls=%fused_computation.2 | loop fusion | flops 3142656 | bytes 12570624 | tf_op jit(solution)/shard_map/stack | solution.py:105
  527.8 7.6 %copy.17843 = bf16[2,33,31,3,512]{4,0,3,2,1:T(2,128)(2,1)} copy(bf16[2,33,31,3,512]{4,3,2,1,0:T(4,128)(2,1)S(1)} %pad_maximum_fusion) | data formatting | bytes 12570624
  (978 shorter events, 116.2 us)
Async XLA Ops:
  7.2 34.0 %copy-start = (f32[16]{0:T(128)S(1)}, f32[16]{0:T(128)}, u32[]{:S(2)}) copy-start(f32[16]{0:T(128)} %param.7) | copy-start | bytes 196
  18.4 22.7 %copy-start.7 = (s32[31]{0:T(128)S(1)}, s32[31]{0:T(128)}, u32[]{:S(2)}) copy-start(s32[31]{0:T(128)} %param.5) | copy-start | bytes 376
  18.4 22.7 %copy-start.6 = (s32[512]{0:T(512)S(1)}, s32[512]{0:T(512)}, u32[]{:S(2)}) copy-start(s32[512]{0:T(512)} %param.6) | copy-start | bytes 6148
  31.8 55.2 %all-to-all-start = ((bf16[16,2,49152]{2,1,0:T(2,128)(2,1)}), bf16[16,2,49152]{2,1,0:T(2,128)(2,1)S(1)}, u32[]{:S(2)}, u32[]{:S(2)}) async-start(bf16[16,2,49152]{2,1,0:T(2,128)(2,1)} %reshape.4626), calls=%async_computation | async-start | bytes 6291456 | tf_op jit(solution)/shard_map/all_to_all | solution.py:110
  40.4 328.7 %all-reduce.4.cloned.1.call-start = ((), (), s32[]{:S(2)}) async-start(), calls=%async_computation.1 | async-start | bytes 2031616 | tf_op jit(solution)/shard_map/psum | solution.py:123
  190.4 9.4 %copy-start.2 = (f32[33,31,1536]{2,1,0:T(8,128)S(1)}, f32[33,31,1536]{2,1,0:T(8,128)}, u32[]{:S(2)}) copy-start(f32[33,31,1536]{2,1,0:T(8,128)} %squeeze.62) | copy-start | bytes 18855940
  190.4 9.4 %copy-start.3 = (f32[33,31,1536]{2,1,0:T(8,128)S(1)}, f32[33,31,1536]{2,1,0:T(8,128)}, u32[]{:S(2)}) copy-start(f32[33,31,1536]{2,1,0:T(8,128)} %squeeze.63) | copy-start | bytes 18855940
  372.6 54.7 %copy-start.4 = (f32[1,31,33]{2,0,1:T(1,128)}, f32[1,31,33]{2,0,1:T(1,128)S(1)}, u32[]{:S(2)}) copy-start(f32[1,31,33]{2,0,1:T(1,128)S(1)} %broadcast_select_fusion.55) | copy-start | bytes 12280
  452.4 8.1 %slice-start.2 = ((f32[1,31,33]{2,0,1:T(1,128)}), f32[1,28,33]{2,0,1:T(1,128)S(1)}, s32[]{:S(2)}) async-start(f32[1,31,33]{2,0,1:T(1,128)} %copy-done.4), calls=%async_computation.4 | async-start | bytes 28672 | tf_op jit(solution)/shard_map/slice | solution.py:83
  466.6 9.6 %copy-start.5 = (f32[31,31,33]{0,1,2:T(8,128)}, f32[31,31,33]{0,1,2:T(8,128)S(1)}, u32[]{:S(2)}) copy-start(f32[31,31,33]{0,1,2:T(8,128)S(1)} %copy.17831) | copy-start | bytes 380560
  477.0 10.2 %slice-start = ((s8[6488064]{0:T(1024)(128)(4,1)}), s8[2293760]{0:T(1024)(128)(4,1)S(1)}, s32[]{:S(2)}) async-start(s8[6488064]{0:T(1024)(128)(4,1)} %bitcast.637), calls=%async_computation.2 | async-start | bytes 4587520
  477.7 9.6 %slice-start.1 = ((s8[6488064]{0:T(1024)(128)(4,1)}), s8[4194304]{0:T(1024)(128)(4,1)S(1)}, s32[]{:S(2)}) async-start(s8[6488064]{0:T(1024)(128)(4,1)} %bitcast.637), calls=%async_computation.3 | async-start | bytes 8388608
  520.2 15.3 %copy-start.1 = (f32[16]{0:T(128)S(1)}, f32[16]{0:T(128)}, u32[]{:S(2)}) copy-start(f32[16]{0:T(128)} %param.7) | copy-start | bytes 196
Sparse Core Ops, SparseCore 0:
  222.0 147.0 all-reduce.3
where the time goes:
time: 550 us; the launch traced here: 543 us
  local copies, waits for them, and re-layouts  208 us (38%)
  waiting for transfers between devices  193 us (35%)
  matrix products  77.3 us (14%)
  other arithmetic  36.3 us (7%)
  between operations  19.3 us (4%)
  starting transfers between devices  8.64 us (2%)
    psum x1, waiting for transfers between devices, on_device(): sum_real, sum_imag = lax.psum((part_real, part_imag), ('pts', 'snap'))  147 us
    unnamed x352, local copies, waits for them, and re-layouts  52.7 us
    all_to_all x1, waiting for transfers between devices, on_device(): lax.all_to_all(snapshots, 'snap', split_axis=2, concat_axis=0, tiled=True)  45.5 us
    slice x3, local copies, waits for them, and re-layouts, gram(): amp_real, amp_imag = (amplitude[0], amplitude[1])  33.9 us
    squeeze x2, local copies, waits for them, and re-layouts, gram(): amp_real, amp_imag = (amplitude[0], amplitude[1])  23.2 us
    another operation x2, local copies, waits for them, and re-layouts, project(): return jnp.stack([mode_real, mode_imag])  14.5 us
    all_to_all x2, local copies, waits for them, and re-layouts, on_device(): lax.all_to_all(snapshots, 'snap', split_axis=2, concat_axis=0, tiled=True)  13 us
    another operation x27, local copies, waits for them, and re-layouts, complex_cholesky(): done_real = jnp.stack(rows_real)  11.6 us
  transfers between devices with their start and end apart: 2, of which 2 were waited for; matrix products, arithmetic and copies ran while one was open for 0% of the time, Pallas kernels for 0%

commit v1 on v0

v1 whole, which is shorter than its diff:
```python
import functools
import math

import jax
import jax.numpy as jnp
import numpy as np
from jax import lax
from jax.experimental import pallas as pl
from jax.experimental.pallas import tpu as pltpu
from jax.sharding import PartitionSpec as P

NT = 1024
WIN = 64
NF = WIN // 2 + 1
NB = 31
PAD = 32
GROUPS = 9
PACK = 4
MIB = 1 << 20


def make_tables(length, freq_count):
    steps_time = jnp.arange(length, dtype=jnp.int32)
    freq_index = jnp.arange(freq_count, dtype=jnp.int32)
    phase_index = freq_index[:, None] * steps_time[None, :] % length
    angle_value = 2.0 * math.pi / length * phase_index.astype(jnp.float32)
    window = 0.5 - 0.5 * jnp.cos(2.0 * math.pi / length * steps_time.astype(jnp.float32))
    dft_table = jnp.stack(
        [window[None, :] * jnp.cos(angle_value), -window[None, :] * jnp.sin(angle_value)]
    ).astype(jnp.bfloat16)
    row_sums = jnp.sum(dft_table.astype(jnp.float32), axis=2)
    return (dft_table, row_sums)


def pack_kernel(x_ref, o_ref):
    o_ref[0] = x_ref[...]


def pack(x, parts):
    comps, steps, width = x.shape
    piece = width // parts
    return pl.pallas_call(
        pack_kernel,
        grid=(parts,),
        in_specs=[pl.BlockSpec((comps, steps, piece), lambda i: (0, 0, i))],
        out_specs=pl.BlockSpec((1, comps, steps, piece), lambda i: (i, 0, 0, 0)),
        out_shape=jax.ShapeDtypeStruct((parts, comps, steps, piece), x.dtype),
        name="pack",
    )(x)


def shift_kernel(starts_ref, table_ref, d_ref):
    steps = lax.broadcasted_iota(jnp.int32, (PAD, NT), 1)
    offset = steps - starts_ref[...]
    index = jnp.where((offset >= 0) & (offset < WIN), offset, WIN)

    def body(f, carry):
        for k in range(2):
            row = jnp.broadcast_to(table_ref[pl.ds(2 * f + k, 1), :], (PAD, 128))
            for tile in range(NT // 128):
                part = index[:, tile * 128 : (tile + 1) * 128]
                value = jnp.take_along_axis(row, part, axis=1, mode="promise_in_bounds")
                d_ref[pl.ds(pl.multiple_of(f * 64 + k * PAD, PAD), PAD), tile * 128 : (tile + 1) * 128] = value.astype(jnp.bfloat16)
        return carry

    lax.fori_loop(0, NF, body, 0)


def shifted_tables(starts, table):
    starts_col = jnp.broadcast_to(
        jnp.concatenate([starts, jnp.full((1,), 2 * NT, jnp.int32)])[:, None], (PAD, NT)
    )
    rows = jnp.zeros((NF * 2, 128), jnp.float32).at[:, :WIN].set(
        jnp.transpose(table, (1, 0, 2)).reshape(NF * 2, WIN).astype(jnp.float32)
    )
    return pl.pallas_call(
        shift_kernel,
        out_shape=jax.ShapeDtypeStruct((NF * 64, NT), jnp.bfloat16),
        compiler_params=pltpu.CompilerParams(vmem_limit_bytes=32 * MIB),
        name="shift_tables",
    )(starts_col, rows)


def spectra_kernel(sums_ref, d_ref, x_ref, root_ref, a_ref, g_ref, s_ref, acc_ref):
    comp = pl.program_id(0)
    series = x_ref[...].reshape(NT, x_ref.shape[3])
    mean = jnp.sum(series.astype(jnp.float32), axis=0, keepdims=True) / NT
    root = root_ref[...]

    @pl.when(comp == 0)
    def _():
        acc_ref[...] = jnp.zeros_like(acc_ref)

    rows = 11 * 64

    def product(i, carry):
        at = pl.ds(pl.multiple_of(i * rows, rows), rows)
        s_ref[at, :] = jnp.dot(d_ref[at, :], series, preferred_element_type=jnp.float32)
        return carry

    lax.fori_loop(0, NF // 11, product, 0)

    def one(f, carry):
        top = s_ref[pl.ds(pl.multiple_of(f * 64, 64), PAD), :]
        low = s_ref[pl.ds(pl.multiple_of(f * 64 + PAD, PAD), PAD), :]
        top = (top - sums_ref[2 * f] * mean) * root
        low = (low - sums_ref[2 * f + 1] * mean) * root
        amp = jnp.concatenate([top, low], axis=0)
        high = amp.astype(jnp.bfloat16)
        rest = (amp - high.astype(jnp.float32)).astype(jnp.bfloat16)
        both = jnp.concatenate([high, rest], axis=0)
        a_ref[0, f] = both
        acc_ref[f] += lax.dot_general(
            both, both, (((1,), (1,)), ((), ())), preferred_element_type=jnp.float32
        )
        return carry

    lax.fori_loop(0, NF, one, 0)

    @pl.when(comp == pl.num_programs(0) - 1)
    def _():
        row = lax.broadcasted_iota(jnp.int32, (PAD, 128), 0)
        lane = lax.broadcasted_iota(jnp.int32, (PAD, 128), 1)

        def packed(f):
            quad = acc_ref[f]
            half = quad[:64] + quad[64:]
            full = half + pltpu.roll(half, 64, 1)
            real = full[:PAD] + pltpu.roll(full[PAD:], 96, 1)
            imag = pltpu.roll(full[:PAD], 96, 1) - full[PAD:]
            return jnp.where(lane < PAD, jnp.where(row <= lane, real, imag), 0.0)

        def group(g, carry):
            total = packed(PACK * g)
            for q in range(1, PACK):
                total = total + pltpu.roll(packed(PACK * g + q), PAD * q, 1)
            g_ref[g] = total
            return carry

        lax.fori_loop(0, GROUPS - 1, group, 0)
        g_ref[GROUPS - 1] = packed(NF - 1)


def spectra_and_gram(sums, tables, series, root):
    parts, comps, steps, width = series.shape
    return pl.pallas_call(
        spectra_kernel,
        grid=(comps,),
        in_specs=[
            pl.BlockSpec(memory_space=pltpu.SMEM),
            pl.BlockSpec((NF * 64, NT), lambda c: (0, 0), pipeline_mode=pl.Buffered(1)),
            pl.BlockSpec((parts, 1, steps, width), lambda c: (0, c, 0, 0)),
            pl.BlockSpec((1, width), lambda c: (0, 0)),
        ],
        out_specs=[
            pl.BlockSpec((1, NF, 128, width), lambda c: (c, 0, 0, 0)),
            pl.BlockSpec((GROUPS, PAD, 128), lambda c: (0, 0, 0)),
        ],
        out_shape=[
            jax.ShapeDtypeStruct((comps, NF, 128, width), jnp.bfloat16),
            jax.ShapeDtypeStruct((GROUPS, PAD, 128), jnp.float32),
        ],
        scratch_shapes=[
            pltpu.VMEM((NF * 64, width), jnp.float32),
            pltpu.VMEM((NF, 128, 128), jnp.float32),
        ],
        compiler_params=pltpu.CompilerParams(vmem_limit_bytes=48 * MIB),
        name="spectra_gram",
    )(sums, tables, series, root)


def factor_kernel(scale, m_ref, w_ref, r_ref, gr_ref, gi_ref, lr_ref, li_ref, mix_ref):
    row = lax.broadcasted_iota(jnp.int32, (PAD, 128), 0)
    lane = lax.broadcasted_iota(jnp.int32, (PAD, 128), 1)
    col = lane % PAD
    block = lane // PAD
    eye = (col == row).astype(jnp.float32)

    for g in range(GROUPS):
        packed = m_ref[g] * scale
        turned = jnp.transpose(jnp.concatenate([packed] * PACK, axis=0))
        other = jnp.where(block == 0, turned[:PAD], 0.0)
        for q in range(1, PACK):
            other = jnp.where(block == q, turned[q * PAD : (q + 1) * PAD], other)
        real = jnp.where(col >= row, packed, other)
        imag = jnp.where(col < row, packed, jnp.where(col > row, -other, 0.0))
        spare = PACK * g + block >= NF
        gr_ref[g] = jnp.where(spare, eye, real)
        gi_ref[g] = jnp.where(spare, 0.0, imag)
        lr_ref[g] = eye
        li_ref[g] = jnp.zeros_like(eye)

    def pick(x, index):
        return jnp.take_along_axis(x, index, axis=1, mode="promise_in_bounds")

    def column(j, carry):
        index = block * PAD + j
        below = row > j
        for g in range(GROUPS):
            real, imag = gr_ref[g], gi_ref[g]
            at = pl.ds(j, 1)
            row_real, row_imag = gr_ref[g, at, :], gi_ref[g, at, :]
            low_real, low_imag = lr_ref[g, at, :], li_ref[g, at, :]
            pivot = pick(jnp.broadcast_to(row_real, (8, 128)), index[:8])[:1]
            inverse = 1.0 / pivot
            mult_real = jnp.where(below, pick(real, index) * inverse, 0.0)
            mult_imag = jnp.where(below, pick(imag, index) * inverse, 0.0)
            gr_ref[g] = real - (mult_real * row_real - mult_imag * row_imag)
            gi_ref[g] = imag - (mult_real * row_imag + mult_imag * row_real)
            lr_ref[g] = lr_ref[g] - (mult_real * low_real - mult_imag * low_imag)
            li_ref[g] = li_ref[g] - (mult_real * low_imag + mult_imag * low_real)
        return carry

    lax.fori_loop(0, NB, column, 0)

    for g in range(GROUPS):
        pivot = pick(gr_ref[g], block * PAD + row)
        root = 1.0 / jnp.sqrt(pivot)
        r_ref[0, g] = jnp.where(col >= row, gr_ref[g] * root, 0.0)
        r_ref[1, g] = jnp.where(col > row, gi_ref[g] * root, 0.0)
        low_real = lr_ref[g] * root
        low_imag = li_ref[g] * root
        for q in range(PACK):
            if PACK * g + q >= NF:
                continue
            real = pltpu.roll(low_real, (128 - PAD * q) % 128, 1)
            imag = pltpu.roll(low_imag, (128 - PAD * q) % 128, 1)
            real_next = pltpu.roll(low_real, (160 - PAD * q) % 128, 1)
            imag_next = pltpu.roll(low_imag, (160 - PAD * q) % 128, 1)
            first = jnp.where(lane < PAD, real, imag_next)
            second = jnp.where(lane < PAD, -imag, real_next)
            mix_ref[pl.ds(0, PAD, stride=2), :] = jnp.where(lane < 64, first, 0.0)
            mix_ref[pl.ds(1, PAD, stride=2), :] = jnp.where(lane < 64, second, 0.0)
            full = mix_ref[...]
            high = full.astype(jnp.bfloat16).astype(jnp.float32)
            rest = full - high
            both = jnp.concatenate(
                [high + pltpu.roll(high, 64, 1), rest + pltpu.roll(rest, 64, 1)], axis=0
            )
            w_ref[PACK * g + q] = both.astype(jnp.bfloat16)


def factor(gram, scale):
    return pl.pallas_call(
        functools.partial(factor_kernel, scale),
        out_shape=[
            jax.ShapeDtypeStruct((NF, 128, 128), jnp.bfloat16),
            jax.ShapeDtypeStruct((2, GROUPS, PAD, 128), jnp.float32),
        ],
        scratch_shapes=[pltpu.VMEM((GROUPS, PAD, 128), jnp.float32)] * 4
        + [pltpu.VMEM((64, 128), jnp.float32)],
        compiler_params=pltpu.CompilerParams(vmem_limit_bytes=32 * MIB),
        name="factor",
    )(gram)


def project_kernel(w_ref, a_ref, o_ref):
    for c in range(a_ref.shape[0]):
        out = jnp.dot(w_ref[0], a_ref[c, 0], preferred_element_type=jnp.float32)
        mode = (out[:64] + out[64:]).astype(jnp.bfloat16)
        o_ref[0, :, c] = mode.reshape(PAD, 2, mode.shape[1])[:NB]


def project(weights, amplitude):
    comps, freqs, rows, width = amplitude.shape
    return pl.pallas_call(
        project_kernel,
        grid=(freqs,),
        in_specs=[
            pl.BlockSpec((1, 128, 128), lambda f: (f, 0, 0)),
            pl.BlockSpec((comps, 1, rows, width), lambda f: (0, f, 0, 0)),
        ],
        out_specs=pl.BlockSpec((1, NB, comps, 2, width), lambda f: (f, 0, 0, 0, 0)),
        out_shape=jax.ShapeDtypeStruct((freqs, NB, comps, 2, width), jnp.bfloat16),
        compiler_params=pltpu.CompilerParams(vmem_limit_bytes=32 * MIB),
        name="project",
    )(weights, amplitude)


def sum_everywhere(x):
    both = ("pts", "snap")
    snap = lax.axis_size("snap")
    count = lax.axis_size("pts") * snap

    def swap(value, mask):
        return lax.ppermute(value, both, [(i, i ^ mask) for i in range(count)])

    half = x.shape[0] // 2
    core = lax.axis_index("pts") % 2
    mine = jnp.where(core == 0, x[:half], x[half:])
    other = jnp.where(core == 0, x[half:], x[:half])
    total = mine + swap(other, snap)
    mask = 1
    while mask < count:
        if mask != snap:
            total = total + swap(total, mask)
        mask *= 2
    rest = swap(total, snap)
    return jnp.where(core == 0, jnp.concatenate([total, rest]), jnp.concatenate([rest, total]))


def on_device(snapshots, block_starts, point_slab, slab_weight):
    dft_table, row_sums = make_tables(WIN, NF)
    parts = lax.axis_size("snap")
    send = pack(jnp.transpose(snapshots, (1, 0, 2)), parts)
    series = lax.all_to_all(send, "snap", split_axis=0, concat_axis=0, tiled=True)
    tables = shifted_tables(block_starts, dft_table)
    comps, points = (series.shape[1], series.shape[3])
    slab_ids = jnp.arange(slab_weight.shape[0], dtype=jnp.int32)
    chosen = jnp.where(point_slab[:, None] == slab_ids[None, :], slab_weight[None, :], 0.0)
    root_weight = jnp.sqrt(jnp.sum(chosen, axis=1) / (0.375 * WIN))
    sums = jnp.transpose(row_sums).reshape(2 * NF)
    amplitude, gram = spectra_and_gram(sums, tables, series, root_weight[None, :])
    all_points = points * lax.axis_size("pts") * lax.axis_size("snap")
    total = sum_everywhere(gram.reshape(GROUPS * PAD, 128)).reshape(GROUPS, PAD, 128)
    weights, upper = factor(total, 1.0 / (comps * all_points))
    mode_field = jnp.transpose(project(weights, amplitude), (3, 0, 1, 2, 4))
    upper = jnp.transpose(upper.reshape(2, GROUPS, PAD, PACK, PAD), (0, 1, 3, 2, 4))
    r_factor = upper.reshape(2, GROUPS * PACK, PAD, PAD)[:, :NF, :NB, :NB]
    return (mode_field, r_factor)


def solution(mesh):
    in_specs = (P("snap", None, "pts"), P(), P(("pts", "snap")), P())
    out_specs = (P(None, None, None, None, ("pts", "snap")), P())
    return jax.shard_map(
        on_device, mesh=mesh, in_specs=in_specs, out_specs=out_specs, check_vma=False
    )
```

time: 550 us -> 188 us (0.34); the launches traced: 543 us -> 187 us
  local copies, waits for them, and re-layouts: 208 us -> 8.91 us
  waiting for transfers between devices: 193 us -> 56.9 us
  Pallas kernels: 0 us -> 94.1 us
  matrix products: 77.3 us -> 0 us
  other arithmetic: 36.3 us -> 2.42 us
  between operations: 19.3 us -> 0.8 us
  starting transfers between devices: 8.64 us -> 24.3 us
    psum x1 -> x0, waiting for transfers between devices: 147 us -> none  [on_device(): sum_real, sum_imag = lax.psum((part_real, part_imag), ('pts', 'snap'))]
    pallas_call x0 -> x5, Pallas kernels: none -> 94.1 us  [the longest x1 34.9 us: spectra_and_gram(): pl.pallas_call(spectra_kernel, grid=(comps,), in_specs=[pl.BlockSpec(memo...]
    dot_general x10 -> x0, matrix products: 77.3 us -> none  [the longest x1 11.4 us: spectra(): jnp.einsum('kfw,bwcp->kfbcp', dft_table, blocks, preferred_element_type=j...]
    another operation x119 -> x2, local copies, waits for them, and re-layouts: 60.7 us -> 0.32 us  [the longest x2 14.5 us: project(): return jnp.stack([mode_real, mode_imag])]
    unnamed x352 -> x11, local copies, waits for them, and re-layouts: 52.7 us -> 8.33 us
    slice x66 -> x1, local copies, waits for them, and re-layouts: 34.1 us -> 0.07 us  [on_device(): r_factor = upper.reshape(2, GROUPS * PACK, PAD, PAD)[:, :NF, :NB, :NB]]
    squeeze x31 -> x0, local copies, waits for them, and re-layouts: 26 us -> none  [the longest x2 23.2 us: gram(): amp_real, amp_imag = (amplitude[0], amplitude[1])]
    ppermute x0 -> x8, waiting for transfers between devices: none -> 20.4 us  [swap(): return lax.ppermute(value, both, [(i, i ^ mask) for i in range(count)])]
  transfers between devices with their start and end apart: 2 -> 9, of which waited for: 2 -> 9; matrix products, arithmetic and copies ran while one was open for 0% -> 1% of each run, Pallas kernels for 0% -> 3%
where the time goes in v1:
time: 188 us; the launch traced here: 187 us
  Pallas kernels  94.1 us (50%)
  waiting for transfers between devices  56.9 us (30%)
  starting transfers between devices  24.3 us (13%)
  local copies, waits for them, and re-layouts  8.91 us (5%)
  other arithmetic  2.42 us (1%)
    all_to_all x1, waiting for transfers between devices, on_device(): lax.all_to_all(send, 'snap', split_axis=0, concat_axis=0, tiled=True)  36.5 us
    pallas_call x1, Pallas kernels, spectra_and_gram(): pl.pallas_call(spectra_kernel, grid=(comps,), in_specs=[pl.BlockSpec(memo...  34.9 us
    pallas_call x1, Pallas kernels, factor(): pl.pallas_call(functools.partial(factor_kernel, scale), out_shape=[jax.Sh...  27.6 us
    ppermute x8, waiting for transfers between devices, swap(): return lax.ppermute(value, both, [(i, i ^ mask) for i in range(count)])  20.4 us
    pallas_call x1, Pallas kernels, project(): pl.pallas_call(project_kernel, grid=(freqs,), in_specs=[pl.BlockSpec((1,...  16.2 us
    ppermute x8, starting transfers between devices, swap(): return lax.ppermute(value, both, [(i, i ^ mask) for i in range(count)])  15.6 us
    pallas_call x1, Pallas kernels, pack(): pl.pallas_call(pack_kernel, grid=(parts,), in_specs=[pl.BlockSpec((comps,...  9.81 us
    all_to_all x1, starting transfers between devices, on_device(): lax.all_to_all(send, 'snap', split_axis=0, concat_axis=0, tiled=True)  8.73 us
  transfers between devices with their start and end apart: 9, of which 9 were waited for; matrix products, arithmetic and copies ran while one was open for 1% of the time, Pallas kernels for 3%

profile of v1, /device:TPU:1, one launch (start us, length us, event | category | flops | bytes accessed | tf_op | source)
XLA Modules:
  0.0 187.4 jit_solution(15743555864545641872)
XLA Ops:
  0.6 9.8 %pack.1 = bf16[16,3,64,512]{3,2,1,0:T(8,128)(2,1)} custom-call(bf16[3,64,8192]{2,1,0:T(8,128)(2,1)} %bitcast.15), custom_call_target="tpu_custom_call" | custom-call | tf_op jit(solution)/shard_map/pack/pallas_call | solution.py:42
  10.4 8.7 %all-to-all-start = ((bf16[16,3,64,512]{3,2,1,0:T(8,128)(2,1)}), bf16[16,3,64,512]{3,2,1,0:T(8,128)(2,1)S(1)}, u32[]{:S(2)}, u32[]{:S(2)}) async-start(bf16[16,3,64,512]{3,2,1,0:T(8,128)(2,1)} %pack.1), calls=%async_computation | async-start | bytes 6291456 | tf_op jit(solution)/shard_map/all_to_all | solution.py:306
  20.5 0.8 fusion
  21.6 5.5 %shift_tables.1.d_ref = bf16[2112,1024]{1,0:T(8,128)(2,1)S(1)} custom-call(s32[32,1024]{1,0:T(8,128)S(1)} %broadcast_in_dim.10.starts_ref, f32[66,128]{1,0:T(8,128)S(1)} %scatter.4.table_ref), custom_call_target="tpu_custom_call" | custom-call | tf_op jit(solution)/shard_map/shift_tables/pallas_call | solution.py:76
  27.2 2.0 %copy-done = bf16[2112,1024]{1,0:T(8,128)(2,1)} copy-done((bf16[2112,1024]{1,0:T(8,128)(2,1)}, bf16[2112,1024]{1,0:T(8,128)(2,1)S(1)}, u32[]{:S(2)}) %copy-start) | copy-done | bytes 4325400
  29.3 36.5 %all-to-all-done.x_ref = bf16[16,3,64,512]{3,2,1,0:T(8,128)(2,1)S(1)} async-done(((bf16[16,3,64,512]{3,2,1,0:T(8,128)(2,1)}), bf16[16,3,64,512]{3,2,1,0:T(8,128)(2,1)S(1)}, u32[]{:S(2)}, u32[]{:S(2)}) %all-to-all-start) | async-done | bytes 3145760 | tf_op jit(solution)/shard_map/all_to_all | solution.py:306
  65.8 34.9 %spectra_gram.1 = (bf16[3,33,128,512]{3,2,1,0:T(8,128)(2,1)}, f32[9,32,128]{2,1,0:T(8,128)S(1)}) custom-call(f32[66]{0:T(128)S(1)} %reshape.196.sums_ref, bf16[2112,1024]{1,0:T(8,128)(2,1)} %copy-done, bf16[16,3,64,512]{3,2,1,0:T(8,128)(2,1)S(1)} %all-to-all-done.x_ref, f32[1,512]{1,0:T(1,128)S(1)} %bitcast.12), custom_call_target="tpu_custom_call" | custom-call | tf_op jit(solution)/shard_map/spectra_gram/pallas_call | solution.py:146
  100.7 1.9 %collective-permute-start = (f32[144,128]{1,0:T(8,128)S(1)}, f32[144,128]{1,0:T(8,128)S(1)}, u32[]{:S(2)}, u32[]{:S(2)}) collective-permute-start(f32[144,128]{1,0:T(8,128)S(1)} %slice_select_fusion), channel_id=1, source_target_pairs={{0,16},{1,17},{2,18},{3,19},{4,20},{5,21},{6,22},{7,23},{8,24},{9,... | collective-permute-start | bytes 221192 | tf_op jit(solution)/shard_map/ppermute | solution.py:286
  102.6 0.9 collective-permute-done
  103.6 3.2 %collective-permute-done.1 = f32[144,128]{1,0:T(8,128)S(1)} collective-permute-done((f32[144,128]{1,0:T(8,128)S(1)}, f32[144,128]{1,0:T(8,128)S(1)}, u32[]{:S(2)}, u32[]{:S(2)}) %collective-permute-start.1) | collective-permute-done | bytes 73760 | tf_op jit(solution)/shard_map/ppermute | solution.py:286
  107.6 4.0 %collective-permute-done.2 = f32[144,128]{1,0:T(8,128)S(1)} collective-permute-done((f32[144,128]{1,0:T(8,128)S(1)}, f32[144,128]{1,0:T(8,128)S(1)}, u32[]{:S(2)}, u32[]{:S(2)}) %collective-permute-start.2) | collective-permute-done | bytes 73760 | tf_op jit(solution)/shard_map/ppermute | solution.py:286
  111.7 3.2 %collective-permute-done.3 = f32[144,128]{1,0:T(8,128)S(1)} collective-permute-done((f32[144,128]{1,0:T(8,128)S(1)}, f32[144,128]{1,0:T(8,128)S(1)}, u32[]{:S(2)}, u32[]{:S(2)}) %collective-permute-start.3) | collective-permute-done | bytes 73760 | tf_op jit(solution)/shard_map/ppermute | solution.py:286
  114.9 1.3 collective-permute-start.4
  116.2 3.8 %collective-permute-done.4 = f32[144,128]{1,0:T(8,128)S(1)} collective-permute-done((f32[144,128]{1,0:T(8,128)S(1)}, f32[144,128]{1,0:T(8,128)S(1)}, u32[]{:S(2)}, u32[]{:S(2)}) %collective-permute-start.4) | collective-permute-done | bytes 73760 | tf_op jit(solution)/shard_map/ppermute | solution.py:286
  120.0 1.3 collective-permute-start.5
  121.3 2.3 %collective-permute-done.5 = f32[144,128]{1,0:T(8,128)S(1)} collective-permute-done((f32[144,128]{1,0:T(8,128)S(1)}, f32[144,128]{1,0:T(8,128)S(1)}, u32[]{:S(2)}, u32[]{:S(2)}) %collective-permute-start.5) | collective-permute-done | bytes 73760 | tf_op jit(solution)/shard_map/ppermute | solution.py:286
  123.6 2.8 %collective-permute-start.6 = (f32[144,128]{1,0:T(8,128)S(1)}, f32[144,128]{1,0:T(8,128)S(1)}, u32[]{:S(2)}, u32[]{:S(2)}) collective-permute-start(f32[144,128]{1,0:T(8,128)S(1)} %add.55), channel_id=1, source_target_pairs={{0,64},{1,65},{2,66},{3,67},{4,68},{5,69},{6,70},{7,71},{8,72},{9,... | collective-permute-start | bytes 221192 | tf_op jit(solution)/shard_map/ppermute | solution.py:286
  126.4 2.1 %collective-permute-done.6 = f32[144,128]{1,0:T(8,128)S(1)} collective-permute-done((f32[144,128]{1,0:T(8,128)S(1)}, f32[144,128]{1,0:T(8,128)S(1)}, u32[]{:S(2)}, u32[]{:S(2)}) %collective-permute-start.6) | collective-permute-done | bytes 73760 | tf_op jit(solution)/shard_map/ppermute | solution.py:286
  128.5 7.3 %collective-permute-start.7 = (f32[144,128]{1,0:T(8,128)S(1)}, f32[144,128]{1,0:T(8,128)S(1)}, u32[]{:S(2)}, u32[]{:S(2)}) collective-permute-start(f32[144,128]{1,0:T(8,128)S(1)} %add.56), channel_id=1, source_target_pairs={{0,16},{1,17},{2,18},{3,19},{4,20},{5,21},{6,22},{7,23},{8,24},{9,... | collective-permute-start | bytes 221192 | tf_op jit(solution)/shard_map/ppermute | solution.py:286
  135.9 0.9 collective-permute-done.7
  136.8 27.6 %factor.1 = (bf16[33,128,128]{2,1,0:T(8,128)(2,1)S(1)}, f32[2,9,32,128]{3,2,1,0:T(8,128)S(1)}) custom-call(f32[9,32,128]{2,1,0:T(8,128)S(1)} %bitcast.11), custom_call_target="tpu_custom_call" | custom-call | tf_op jit(solution)/shard_map/factor/pallas_call | solution.py:244
  164.9 1.6 copy.19
  166.5 4.7 %copy-done.1 = bf16[3,33,128,512]{3,2,1,0:T(8,128)(2,1)S(1)} copy-done((bf16[3,33,128,512]{3,2,1,0:T(8,128)(2,1)S(1)}, bf16[3,33,128,512]{3,2,1,0:T(8,128)(2,1)}, u32[]{:S(2)}) %copy-start.1) | copy-done | bytes 12976152
  171.2 16.2 %project.1 = bf16[33,31,3,2,512]{4,3,2,1,0:T(2,128)(2,1)} custom-call(bf16[33,128,128]{2,1,0:T(8,128)(2,1)S(1)} %get-tuple-element.19.w_ref, bf16[3,33,128,512]{3,2,1,0:T(8,128)(2,1)S(1)} %copy-done.1), custom_call_target="tpu_custom_call" | custom-call | tf_op jit(solution)/shard_map/project/pallas_call | solution.py:266
  (34 shorter events, 3.2 us)
Async XLA Ops:
  10.4 11.0 %copy-start.4 = (s32[31]{0:T(128)S(1)}, s32[31]{0:T(128)}, u32[]{:S(2)}) copy-start(s32[31]{0:T(128)} %param.7) | copy-start | bytes 376
  10.4 55.4 %all-to-all-start = ((bf16[16,3,64,512]{3,2,1,0:T(8,128)(2,1)}), bf16[16,3,64,512]{3,2,1,0:T(8,128)(2,1)S(1)}, u32[]{:S(2)}, u32[]{:S(2)}) async-start(bf16[16,3,64,512]{3,2,1,0:T(8,128)(2,1)} %pack.1), calls=%async_computation | async-start | bytes 6291456 | tf_op jit(solution)/shard_map/all_to_all | solution.py:306
  21.6 7.6 %copy-start.2 = (s32[512]{0:T(512)S(1)}, s32[512]{0:T(512)}, u32[]{:S(2)}) copy-start(s32[512]{0:T(512)} %param.8) | copy-start | bytes 6148
  21.6 7.6 %copy-start.3 = (f32[16]{0:T(128)S(1)}, f32[16]{0:T(128)}, u32[]{:S(2)}) copy-start(f32[16]{0:T(128)} %param.9) | copy-start | bytes 196
  27.1 2.1 %copy-start = (bf16[2112,1024]{1,0:T(8,128)(2,1)}, bf16[2112,1024]{1,0:T(8,128)(2,1)S(1)}, u32[]{:S(2)}) copy-start(bf16[2112,1024]{1,0:T(8,128)(2,1)S(1)} %shift_tables.1.d_ref) | copy-start | bytes 12976132
  100.7 2.8 %collective-permute-start = (f32[144,128]{1,0:T(8,128)S(1)}, f32[144,128]{1,0:T(8,128)S(1)}, u32[]{:S(2)}, u32[]{:S(2)}) collective-permute-start(f32[144,128]{1,0:T(8,128)S(1)} %slice_select_fusion), channel_id=1, source_target_pairs={{0,16},{1,17},{2,18},{3,19},{4,20},{5,21},{6,22},{7,23},{8,24},{9,... | collective-permute-start | bytes 221192 | tf_op jit(solution)/shard_map/ppermute | solution.py:286
  103.5 3.3 %collective-permute-start.1 = (f32[144,128]{1,0:T(8,128)S(1)}, f32[144,128]{1,0:T(8,128)S(1)}, u32[]{:S(2)}, u32[]{:S(2)}) collective-permute-start(f32[144,128]{1,0:T(8,128)S(1)} %select_add_fusion), channel_id=1, source_target_pairs={{0,1},{1,0},{2,3},{3,2},{4,5},{5,4},{6,7},{7,6},{8,9},{9,8},{10,11... | collective-permute-start | bytes 221192 | tf_op jit(solution)/shard_map/ppermute | solution.py:286
  106.8 4.8 %collective-permute-start.2 = (f32[144,128]{1,0:T(8,128)S(1)}, f32[144,128]{1,0:T(8,128)S(1)}, u32[]{:S(2)}, u32[]{:S(2)}) collective-permute-start(f32[144,128]{1,0:T(8,128)S(1)} %add.51), channel_id=1, source_target_pairs={{0,2},{1,3},{2,0},{3,1},{4,6},{5,7},{6,4},{7,5},{8,10},{9,11},{10,... | collective-permute-start | bytes 221192 | tf_op jit(solution)/shard_map/ppermute | solution.py:286
  111.6 3.3 %collective-permute-start.3 = (f32[144,128]{1,0:T(8,128)S(1)}, f32[144,128]{1,0:T(8,128)S(1)}, u32[]{:S(2)}, u32[]{:S(2)}) collective-permute-start(f32[144,128]{1,0:T(8,128)S(1)} %add.52), channel_id=1, source_target_pairs={{0,4},{1,5},{2,6},{3,7},{4,0},{5,1},{6,2},{7,3},{8,12},{9,13},{10,... | collective-permute-start | bytes 221192 | tf_op jit(solution)/shard_map/ppermute | solution.py:286
  114.9 5.1 %collective-permute-start.4 = (f32[144,128]{1,0:T(8,128)S(1)}, f32[144,128]{1,0:T(8,128)S(1)}, u32[]{:S(2)}, u32[]{:S(2)}) collective-permute-start(f32[144,128]{1,0:T(8,128)S(1)} %add.53), channel_id=1, source_target_pairs={{0,8},{1,9},{2,10},{3,11},{4,12},{5,13},{6,14},{7,15},{8,0},{9,1},... | collective-permute-start | bytes 221192 | tf_op jit(solution)/shard_map/ppermute | solution.py:286
  120.0 3.6 %collective-permute-start.5 = (f32[144,128]{1,0:T(8,128)S(1)}, f32[144,128]{1,0:T(8,128)S(1)}, u32[]{:S(2)}, u32[]{:S(2)}) collective-permute-start(f32[144,128]{1,0:T(8,128)S(1)} %add.54), channel_id=1, source_target_pairs={{0,32},{1,33},{2,34},{3,35},{4,36},{5,37},{6,38},{7,39},{8,40},{9,... | collective-permute-start | bytes 221192 | tf_op jit(solution)/shard_map/ppermute | solution.py:286
  123.6 4.9 %collective-permute-start.6 = (f32[144,128]{1,0:T(8,128)S(1)}, f32[144,128]{1,0:T(8,128)S(1)}, u32[]{:S(2)}, u32[]{:S(2)}) collective-permute-start(f32[144,128]{1,0:T(8,128)S(1)} %add.55), channel_id=1, source_target_pairs={{0,64},{1,65},{2,66},{3,67},{4,68},{5,69},{6,70},{7,71},{8,72},{9,... | collective-permute-start | bytes 221192 | tf_op jit(solution)/shard_map/ppermute | solution.py:286
  128.5 8.3 %collective-permute-start.7 = (f32[144,128]{1,0:T(8,128)S(1)}, f32[144,128]{1,0:T(8,128)S(1)}, u32[]{:S(2)}, u32[]{:S(2)}) collective-permute-start(f32[144,128]{1,0:T(8,128)S(1)} %add.56), channel_id=1, source_target_pairs={{0,16},{1,17},{2,18},{3,19},{4,20},{5,21},{6,22},{7,23},{8,24},{9,... | collective-permute-start | bytes 221192 | tf_op jit(solution)/shard_map/ppermute | solution.py:286
  166.5 4.7 %copy-start.1 = (bf16[3,33,128,512]{3,2,1,0:T(8,128)(2,1)S(1)}, bf16[3,33,128,512]{3,2,1,0:T(8,128)(2,1)}, u32[]{:S(2)}) copy-start(bf16[3,33,128,512]{3,2,1,0:T(8,128)(2,1)} %get-tuple-element.20.a_ref) | copy-start | bytes 38928388
